TPU v7x, 32 devices: a whole 2x2x4 slice. The times are simulated.
32 devices in a mesh: win: 2 (over x), wide: 8 (over z, y), narrow: 2 (over core).
Axes of the slice: x: 2, y: 2, z: 4, core: 2. Of those that a mesh axis runs over, the one named last changes fastest.
Arguments:
- window_data: float32 [384, 128, 256], P(('win', 'wide'), 'narrow'), parts along dimension 0, may hold values from -6 to 6
- factor_one: float32 [256, 48], P(('win', 'narrow')), parts along dimension 0, may hold values from -0.5 to 0.5
- factor_two: float32 [512, 48], P('win'), parts along dimension 0, may hold values from -0.375 to 0.375
- factor_three: float32 [384, 48], P(('win', 'wide')), parts along dimension 0, may hold values from -0.4375 to 0.4375
Outputs:
- basis_one: float32 [256, 48], P(('win', 'narrow')), parts along dimension 0
- basis_two: float32 [512, 48], P('win'), parts along dimension 0
- basis_three: float32 [384, 48], P(('win', 'wide')), parts along dimension 0
- core_unfolded: float32 [48, 4608], P(None, ('win', 'wide', 'narrow')), parts along dimension 1
There are 2 independent parts, one for each index of `win`. A program takes and returns all parts, laid end to end along the dimension named above; each array names one. Nothing has to cross between parts.
All inputs are finite; a program needn't handle non-finite values.
Results may differ from a plain program's by a relative error of at most 0.0003.
Values sent between devices are 32-bit elements; how exact they have to be, the bound alone decides.
No kernel may reach another device: no remote copies, remote signals or barrier semaphores. Data moves between devices by JAX's collectives and lax.ppermute only.
A program may use at most 64 MiB of HBM per device.

v0:
```python
import jax
import jax.numpy as jnp
from jax import lax
from jax.sharding import PartitionSpec as P

highest = lax.Precision.HIGHEST


def contract(form, left, right):
    return jnp.einsum(form, left, right, precision=highest)


def orthonormal(basis, gram):
    lower = jnp.linalg.cholesky(gram)
    return lax.linalg.triangular_solve(lower, basis, left_side=False, lower=True, transpose_a=True)


def full_core(partial_value):
    flat = partial_value.reshape(
        partial_value.shape[0], partial_value.shape[1] * partial_value.shape[2]
    )
    shares = lax.psum_scatter(flat, ("wide", "narrow"), scatter_dimension=1, tiled=True)
    whole = lax.all_gather(shares, ("wide", "narrow"), axis=1, tiled=True)
    return whole.reshape(partial_value.shape)


def on_device(window_data, factor_one, factor_two, factor_three):
    rank = factor_one.shape[1]
    along_two = contract("kij,jb->kib", window_data, factor_two)
    unfold_part = contract("kib,kc->ibc", along_two, factor_three).reshape(
        along_two.shape[1], rank * rank
    )
    unfold_rows = lax.psum_scatter(unfold_part, "wide", scatter_dimension=1, tiled=True)
    weights_one = lax.psum(jnp.dot(unfold_rows.T, factor_one, precision=highest), "narrow")
    product_one = lax.psum(jnp.dot(unfold_rows, weights_one, precision=highest), "wide")
    gram_one = lax.psum(jnp.dot(product_one.T, product_one, precision=highest), "narrow")
    basis_one = orthonormal(product_one, gram_one)
    along_one = contract("kij,ia->kaj", window_data, basis_one)
    core_two = full_core(
        contract("kab,kc->abc", contract("kaj,jb->kab", along_one, factor_two), factor_three)
    )
    spread_two = contract("abc,kc->kab", core_two, factor_three)
    product_two = lax.psum(contract("kaj,kab->jb", along_one, spread_two), ("wide", "narrow"))
    basis_two = orthonormal(product_two, jnp.dot(product_two.T, product_two, precision=highest))
    along_new = contract("kij,jb->kib", window_data, basis_two)
    unfold_three = contract("kib,ia->kab", along_new, basis_one)
    core_three = full_core(contract("kab,kc->abc", unfold_three, factor_three))
    product_three = lax.psum(contract("kab,abc->kc", unfold_three, core_three), "narrow")
    gram_three = lax.psum(jnp.dot(product_three.T, product_three, precision=highest), "wide")
    basis_three = orthonormal(product_three, gram_three)
    core_part = contract("kab,kc->abc", unfold_three, basis_three).reshape(rank, rank * rank)
    core_shares = lax.psum_scatter(core_part, ("wide", "narrow"), scatter_dimension=1, tiled=True)
    return (basis_one, basis_two, basis_three, core_shares)


def solution(mesh):
    return jax.shard_map(
        on_device,
        mesh=mesh,
        in_specs=(
            P(("win", "wide"), "narrow", None),
            P(("win", "narrow"), None),
            P("win", None),
            P(("win", "wide"), None),
        ),
        out_specs=(
            P(("win", "narrow"), None),
            P("win", None),
            P(("win", "wide"), None),
            P(None, ("win", "wide", "narrow")),
        ),
        check_vma=False,
    )
```

profile of v0, /device:TPU:0, one launch (start us, length us, event | category | flops | bytes accessed | tf_op | source)
XLA Modules:
  0.0 505.6 jit_solution(5925950153966513324)
XLA Ops:
  7.2 0.0 reduce-scatter.11.cloned.1.call-start
  7.2 1.3 copy-done
  8.6 3.1 fusion.12
  11.7 2.2 fusion.3
  13.9 0.0 reduce-scatter.13.cloned.1.call-start
  13.9 67.9 %reduce-scatter.11.cloned.1.call-done = f32[64,288]{0,1:T(8,128)} async-done(((f32[64,2304]{0,1:T(8,128)}), f32[64,288]{0,1:T(8,128)}) %reduce-scatter.11.cloned.1.call-update) | async-done | bytes 73744 | tf_op jit(solution)/shard_map/reduce_scatter | solution.py:33
  81.9 1.2 fusion.34
  83.1 3.5 psum.42
  86.6 1.1 fusion.35
  87.7 34.9 %psum.43 = f32[64,48]{0,1:T(8,128)S(1)} all-reduce(f32[64,48]{0,1:T(8,128)S(1)} %fusion.35), channel_id=1, replica_groups=mesh['win'=2,'wide'=8,'narrow'=2] {'wide'}, use_global_device_ids=true, to_apply=%region_2.0 | all-reduce | flops 3072 | bytes 24576 | tf_op jit(solution)/shard_map/psum | solution.py:35
  122.6 0.2 fusion.36
  122.8 3.4 psum.44
  126.2 0.1 copy.26
  126.3 4.4 cholesky.59
  130.7 0.6 compare_reduce_fusion.2
  131.4 0.7 fusion.14
  132.0 3.7 custom-call.11
  135.7 0.2 fusion.25
  136.0 1.1 convolution_bitcast_fusion
  137.1 1.6 fusion
  138.7 3.1 fusion.31
  141.8 2.7 copy.45
  144.5 0.0 reduce-scatter.15.cloned.1.call-start
  144.6 55.5 %reduce-scatter.13.cloned.1.call-done = f32[144,48]{1,0:T(8,128)} async-done(((f32[2304,48]{1,0:T(8,128)}), f32[144,48]{1,0:T(8,128)}) %reduce-scatter.13.cloned.1.call-update) | async-done | bytes 27664
  200.1 1.0 copy.40
  201.0 21.8 %all-gather = f32[16,144,48]{1,2,0:T(8,128)S(1)} all-gather(f32[1,144,48]{1,2,0:T(8,128)S(1)} %bitcast.116), channel_id=1, replica_groups=mesh['win'=2,'wide'=8,'narrow'=2] {'wide','narrow'}, dimensions={0}, use_global_device_ids=true | all-gather | bytes 470016 | tf_op jit(solution)/shard_map/all_gather | solution.py:23
  222.8 0.5 copy.28
  223.3 1.2 reshape.47
  224.4 2.7 reshape.42
  227.2 4.7 convolution_bitcast_fusion.3
  231.9 1.2 convolution_bitcast_fusion.4
  233.1 57.9 %psum.45 = f32[256,48]{0,1:T(8,128)S(1)} all-reduce(f32[256,48]{0,1:T(8,128)S(1)} %convolution_bitcast_fusion.4), channel_id=1, replica_groups=mesh['win'=2,'wide'=8,'narrow'=2] {'wide','narrow'}, use_global_device_ids=true, to_apply=%region_7.0 | all-reduce | flops 12288 | bytes 98304 | tf_op jit(solution)/shard_map/psum | solution.py:43
  291.0 0.2 fusion.37
  291.2 0.1 copy.30
  291.3 4.4 cholesky.70
  295.7 0.6 compare_reduce_fusion.1
  296.4 0.7 fusion.15
  297.0 3.7 custom-call.12
  300.7 0.2 fusion.20
  301.0 2.3 convolution_bitcast_fusion.2
  303.3 2.1 convolution_bitcast_fusion.1
  305.5 2.0 fusion.7
  307.5 1.5 copy.46
  309.0 0.0 reduce-scatter.17.cloned.1.call-start
  309.1 55.5 %reduce-scatter.15.cloned.1.call-done = f32[144,48]{1,0:T(8,128)} async-done(((f32[2304,48]{1,0:T(8,128)}), f32[144,48]{1,0:T(8,128)}) %reduce-scatter.15.cloned.1.call-update) | async-done | bytes 27664
  364.6 1.0 copy.42
  365.5 21.8 %all-gather.1 = f32[16,144,48]{1,2,0:T(8,128)S(1)} all-gather(f32[1,144,48]{1,2,0:T(8,128)S(1)} %bitcast.117), channel_id=1, replica_groups=mesh['win'=2,'wide'=8,'narrow'=2] {'wide','narrow'}, dimensions={0}, use_global_device_ids=true | all-gather | bytes 470016 | tf_op jit(solution)/shard_map/all_gather | solution.py:23
  387.3 0.5 copy.32
  387.8 1.1 reshape.49
  388.9 1.7 reshape.44
  390.7 1.2 convolution_bitcast_fusion.5
  391.9 3.5 psum.46
  395.4 0.2 fusion.38
  395.6 33.0 %psum.47 = f32[48,48]{0,1:T(8,128)S(1)} all-reduce(f32[48,48]{0,1:T(8,128)S(1)} %fusion.38), channel_id=1, replica_groups=mesh['win'=2,'wide'=8,'narrow'=2] {'wide'}, use_global_device_ids=true, to_apply=%region_10.12 | all-reduce | flops 2304 | bytes 18432 | tf_op jit(solution)/shard_map/psum | solution.py:49
  428.6 0.1 copy.35
  428.7 4.4 cholesky.81
  433.1 0.6 compare_reduce_fusion
  433.8 0.7 fusion.16
  434.4 3.7 custom-call.13
  438.1 0.2 fusion.17
  438.3 2.0 fusion.5
  440.3 1.5 copy.47
  441.9 55.6 %reduce-scatter.17.cloned.1.call-done = f32[144,48]{1,0:T(8,128)} async-done(((f32[2304,48]{1,0:T(8,128)}), f32[144,48]{1,0:T(8,128)}) %reduce-scatter.17.cloned.1.call-update) | async-done | bytes 27664
  497.5 1.6 copy.44
  (25 shorter events, 0.2 us)
Async XLA Ops:
  7.2 1.4 copy-start
  7.2 4.5 copy-start.3
  7.2 74.7 %reduce-scatter.11.cloned.1.call-start = ((), (), s32[]{:S(2)}) async-start(), calls=%async_computation.4 | async-start | bytes 1327104 | tf_op jit(solution)/shard_map/reduce_scatter | solution.py:33
  11.7 70.2 %copy-start.7 = (f32[64,48]{0,1:T(8,128)S(1)}, f32[64,48]{0,1:T(8,128)}, u32[]{:S(2)}) copy-start(f32[64,48]{0,1:T(8,128)} %param.6) | copy-start | bytes 36868
  13.9 186.2 %reduce-scatter.13.cloned.1.call-start = ((), (), s32[]{:S(2)}) async-start(), calls=%async_computation.5 | async-start | bytes 1253376
  135.9 1.1 copy-start.1
  136.0 1.1 copy-start.5
  144.5 220.0 %reduce-scatter.15.cloned.1.call-start = ((), (), s32[]{:S(2)}) async-start(), calls=%async_computation.6 | async-start | bytes 1253376
  297.0 6.3 %copy-start.2 = (f32[64,48]{0,1:T(8,128)S(1)}, f32[64,48]{0,1:T(8,128)}, u32[]{:S(2)}) copy-start(f32[64,48]{0,1:T(8,128)} %copy-done.1) | copy-start | bytes 36868
  301.0 4.5 copy-start.4
  309.0 188.4 %reduce-scatter.17.cloned.1.call-start = ((), (), s32[]{:S(2)}) async-start(), calls=%async_computation.7 | async-start | bytes 1253376
  438.3 3.6 copy-start.6
Sparse Core Ops, SparseCore 0:
  14.0 67.8 reduce-scatter.10
  144.7 55.3 reduce-scatter.12
  309.1 55.3 reduce-scatter.14
  442.0 55.4 reduce-scatter.16
where the time goes:
time: 506 us
  waiting for transfers between devices  235 us (46%)
  blocking collectives  180 us (36%)
  matrix products  30.3 us (6%)
  other arithmetic  28.2 us (6%)
  local copies, waits for them, and re-layouts  18.5 us (4%)
  between operations  14.1 us (3%)
    unnamed x7, waiting for transfers between devices  167 us
    reduce_scatter x1, waiting for transfers between devices, on_device(): lax.psum_scatter(unfold_part, 'wide', scatter_dimension=1, tiled=True)  67.9 us
    psum x1, blocking collectives, on_device(): lax.psum(contract('kaj,kab->jb', along_one, spread_two), ('wide', 'narrow'))  57.9 us
    all_gather x2, blocking collectives, full_core(): whole = lax.all_gather(shares, ('wide', 'narrow'), axis=1, tiled=True)  43.6 us
    psum x1, blocking collectives, on_device(): lax.psum(jnp.dot(unfold_rows, weights_one, precision=highest), 'wide')  34.9 us
    psum x1, blocking collectives, on_device(): lax.psum(jnp.dot(product_three.T, product_three, precision=highest), 'wide')  33 us
    dot_general x12, matrix products, contract(): return jnp.einsum(form, left, right, precision=highest)  26.7 us
    another operation x9, other arithmetic, orthonormal(): lower = jnp.linalg.cholesky(gram)  15.2 us
  transfers between devices with their start and end apart: 4, of which 4 were waited for; matrix products, arithmetic and copies ran while one was open for 0% of the time, Pallas kernels for 0%

commit v1 on v0

--- a/solution.py
+++ b/solution.py
@@ -40,7 +40,9 @@
         contract("kab,kc->abc", contract("kaj,jb->kab", along_one, factor_two), factor_three)
     )
     spread_two = contract("abc,kc->kab", core_two, factor_three)
-    product_two = lax.psum(contract("kaj,kab->jb", along_one, spread_two), ("wide", "narrow"))
+    product_two = lax.psum(
+        lax.psum(contract("kaj,kab->jb", along_one, spread_two), "wide"), "narrow"
+    )
     basis_two = orthonormal(product_two, jnp.dot(product_two.T, product_two, precision=highest))
     along_new = contract("kij,jb->kib", window_data, basis_two)
     unfold_three = contract("kib,ia->kab", along_new, basis_one)

time: 506 us -> 487 us (0.962)
  blocking collectives: 180 us -> 159 us
    psum x1 -> x2, blocking collectives: 57.9 us -> 36.9 us  [the longest x1 33.4 us: on_device(): lax.psum(contract('kaj,kab->jb', along_one, spread_two), 'wide')]
where the time goes in v1:
time: 487 us; the launch traced here: 486 us
  waiting for transfers between devices  236 us (48%)
  blocking collectives  159 us (33%)
  matrix products  30.3 us (6%)
  other arithmetic  28.2 us (6%)
  local copies, waits for them, and re-layouts  18.5 us (4%)
  between operations  14.1 us (3%)
    unnamed x7, waiting for transfers between devices  168 us
    reduce_scatter x1, waiting for transfers between devices, on_device(): lax.psum_scatter(unfold_part, 'wide', scatter_dimension=1, tiled=True)  67.9 us
    all_gather x2, blocking collectives, full_core(): whole = lax.all_gather(shares, ('wide', 'narrow'), axis=1, tiled=True)  43.3 us
    psum x1, blocking collectives, on_device(): lax.psum(jnp.dot(unfold_rows, weights_one, precision=highest), 'wide')  34.9 us
    psum x1, blocking collectives, on_device(): lax.psum(contract('kaj,kab->jb', along_one, spread_two), 'wide')  33.4 us
    psum x1, blocking collectives, on_device(): lax.psum(jnp.dot(product_three.T, product_three, precision=highest), 'wide')  33 us
    dot_general x12, matrix products, contract(): return jnp.einsum(form, left, right, precision=highest)  26.7 us
    another operation x9, other arithmetic, orthonormal(): lower = jnp.linalg.cholesky(gram)  15.2 us
  transfers between devices with their start and end apart: 4, of which 4 were waited for; matrix products, arithmetic and copies ran while one was open for 0% of the time, Pallas kernels for 0%

profile of v1, /device:TPU:0, one launch (start us, length us, event | category | flops | bytes accessed | tf_op | source)
XLA Modules:
  0.0 485.8 jit_solution(5804607225270512968)
XLA Ops:
  7.2 1.3 copy-done
  8.6 3.1 fusion.12
  11.7 2.2 fusion.3
  13.9 0.0 reduce-scatter.13.cloned.1.call-start
  13.9 67.9 %reduce-scatter.11.cloned.1.call-done = f32[64,288]{0,1:T(8,128)} async-done(((f32[64,2304]{0,1:T(8,128)}), f32[64,288]{0,1:T(8,128)}) %reduce-scatter.11.cloned.1.call-update) | async-done | bytes 73744 | tf_op jit(solution)/shard_map/reduce_scatter | solution.py:33
  81.9 1.2 fusion.34
  83.1 3.5 psum.49
  86.6 1.1 fusion.35
  87.7 34.9 %psum.50 = f32[64,48]{0,1:T(8,128)S(1)} all-reduce(f32[64,48]{0,1:T(8,128)S(1)} %fusion.35), channel_id=1, replica_groups=mesh['win'=2,'wide'=8,'narrow'=2] {'wide'}, use_global_device_ids=true, to_apply=%region_2.0 | all-reduce | flops 3072 | bytes 24576 | tf_op jit(solution)/shard_map/psum | solution.py:35
  122.6 0.2 fusion.36
  122.8 3.4 psum.51
  126.2 0.1 copy.26
  126.3 4.4 cholesky.59
  130.7 0.6 compare_reduce_fusion.2
  131.4 0.7 fusion.14
  132.0 3.7 custom-call.11
  135.7 0.2 fusion.25
  136.0 1.1 convolution_bitcast_fusion
  137.1 1.6 fusion
  138.7 3.1 fusion.31
  141.8 2.7 copy.45
  144.5 0.0 reduce-scatter.15.cloned.1.call-start
  144.6 55.5 %reduce-scatter.13.cloned.1.call-done = f32[144,48]{1,0:T(8,128)} async-done(((f32[2304,48]{1,0:T(8,128)}), f32[144,48]{1,0:T(8,128)}) %reduce-scatter.13.cloned.1.call-update) | async-done | bytes 27664
  200.1 1.0 copy.40
  201.0 21.8 %all-gather = f32[16,144,48]{1,2,0:T(8,128)S(1)} all-gather(f32[1,144,48]{1,2,0:T(8,128)S(1)} %bitcast.116), channel_id=1, replica_groups=mesh['win'=2,'wide'=8,'narrow'=2] {'wide','narrow'}, dimensions={0}, use_global_device_ids=true | all-gather | bytes 470016 | tf_op jit(solution)/shard_map/all_gather | solution.py:23
  222.8 0.5 copy.28
  223.3 1.2 reshape.47
  224.4 2.7 reshape.42
  227.2 4.7 convolution_bitcast_fusion.3
  231.9 1.2 convolution_bitcast_fusion.4
  233.1 33.4 %psum.52 = f32[256,48]{0,1:T(8,128)S(1)} all-reduce(f32[256,48]{0,1:T(8,128)S(1)} %convolution_bitcast_fusion.4), channel_id=1, replica_groups=mesh['win'=2,'wide'=8,'narrow'=2] {'wide'}, use_global_device_ids=true, to_apply=%region_7.0 | all-reduce | flops 12288 | bytes 98304 | tf_op jit(solution)/shard_map/psum | solution.py:44
  266.5 3.5 psum.53
  270.0 0.2 fusion.37
  270.2 0.1 copy.30
  270.3 4.4 cholesky.70
  274.7 0.6 compare_reduce_fusion.1
  275.4 0.7 fusion.15
  276.1 3.7 custom-call.12
  279.7 0.3 fusion.20
  280.0 2.3 convolution_bitcast_fusion.2
  282.3 2.1 convolution_bitcast_fusion.1
  284.5 2.0 fusion.7
  286.5 1.5 copy.46
  288.0 0.3 reduce-scatter.17.cloned.1.call-start
  288.3 56.7 %reduce-scatter.15.cloned.1.call-done = f32[144,48]{1,0:T(8,128)} async-done(((f32[2304,48]{1,0:T(8,128)}), f32[144,48]{1,0:T(8,128)}) %reduce-scatter.15.cloned.1.call-update) | async-done | bytes 27664
  345.0 1.0 copy.42
  346.0 21.6 %all-gather.1 = f32[16,144,48]{1,2,0:T(8,128)S(1)} all-gather(f32[1,144,48]{1,2,0:T(8,128)S(1)} %bitcast.117), channel_id=1, replica_groups=mesh['win'=2,'wide'=8,'narrow'=2] {'wide','narrow'}, dimensions={0}, use_global_device_ids=true | all-gather | bytes 470016 | tf_op jit(solution)/shard_map/all_gather | solution.py:23
  367.6 0.5 copy.32
  368.0 1.1 reshape.49
  369.2 1.7 reshape.44
  370.9 1.2 convolution_bitcast_fusion.5
  372.2 3.5 psum.54
  375.6 0.2 fusion.38
  375.9 33.0 %psum.55 = f32[48,48]{0,1:T(8,128)S(1)} all-reduce(f32[48,48]{0,1:T(8,128)S(1)} %fusion.38), channel_id=1, replica_groups=mesh['win'=2,'wide'=8,'narrow'=2] {'wide'}, use_global_device_ids=true, to_apply=%region_11.13 | all-reduce | flops 2304 | bytes 18432 | tf_op jit(solution)/shard_map/psum | solution.py:51
  408.9 0.1 copy.35
  409.0 4.4 cholesky.81
  413.4 0.6 compare_reduce_fusion
  414.0 0.7 fusion.16
  414.7 3.7 custom-call.13
  418.4 0.2 fusion.17
  418.6 2.0 fusion.5
  420.6 1.5 copy.47
  422.1 55.6 %reduce-scatter.17.cloned.1.call-done = f32[144,48]{1,0:T(8,128)} async-done(((f32[2304,48]{1,0:T(8,128)}), f32[144,48]{1,0:T(8,128)}) %reduce-scatter.17.cloned.1.call-update) | async-done | bytes 27664
  477.7 1.6 copy.44
  (26 shorter events, 0.3 us)
Async XLA Ops:
  7.2 1.4 copy-start
  7.2 4.5 copy-start.3
  7.2 74.7 %reduce-scatter.11.cloned.1.call-start = ((), (), s32[]{:S(2)}) async-start(), calls=%async_computation.4 | async-start | bytes 1327104 | tf_op jit(solution)/shard_map/reduce_scatter | solution.py:33
  11.7 70.2 %copy-start.7 = (f32[64,48]{0,1:T(8,128)S(1)}, f32[64,48]{0,1:T(8,128)}, u32[]{:S(2)}) copy-start(f32[64,48]{0,1:T(8,128)} %param.6) | copy-start | bytes 36868
  13.9 186.2 %reduce-scatter.13.cloned.1.call-start = ((), (), s32[]{:S(2)}) async-start(), calls=%async_computation.5 | async-start | bytes 1253376
  135.9 1.1 copy-start.1
  136.0 1.1 copy-start.5
  144.5 200.5 %reduce-scatter.15.cloned.1.call-start = ((), (), s32[]{:S(2)}) async-start(), calls=%async_computation.6 | async-start | bytes 1253376
  276.0 6.3 %copy-start.2 = (f32[64,48]{0,1:T(8,128)S(1)}, f32[64,48]{0,1:T(8,128)}, u32[]{:S(2)}) copy-start(f32[64,48]{0,1:T(8,128)} %copy-done.1) | copy-start | bytes 36868
  280.0 4.5 copy-start.4
  288.0 189.7 %reduce-scatter.17.cloned.1.call-start = ((), (), s32[]{:S(2)}) async-start(), calls=%async_computation.7 | async-start | bytes 1253376
  418.5 3.6 copy-start.6
Sparse Core Ops, SparseCore 0:
  14.0 67.8 reduce-scatter.10
  144.7 55.3 reduce-scatter.12
  288.2 56.8 reduce-scatter.14
  422.2 55.4 reduce-scatter.16
